TPU v7x, 32 devices: a whole 2x2x4 slice. The times are simulated.
32 devices in a mesh: blocks: 8 (over z, x), span: 4 (over y, core).
Axes of the slice: x: 2, y: 2, z: 4, core: 2. Of those that a mesh axis runs over, the one named last changes fastest.
Arguments:
- struct_disp: float32 [3, 16384], P(None, ('blocks', 'span')), may hold values from -3 to 3
- rec_struct: int32 [16384], P(('blocks', 'span')), may hold values from 0 to 511
- rec_block: int32 [16384, 1], P(('blocks', 'span')), may hold values from 0 to 7; in each aligned block of 512 rows (0 to 511, 512 to 1023, ...) at most 128 rows name the same one
- rec_node: int32 [16384], P(('blocks', 'span')), may hold values from 0 to 8191
- rec_weight: float32 [16384], P(('blocks', 'span')), may hold values from 0.2 to 1
- offset: float32 [3, 16, 256, 1024], P(None, None, 'blocks', 'span'), may hold values from -0.6 to 0.6
- prior_warp: float32 [3, 16, 256, 1024], P(None, None, 'blocks', 'span'), may hold values from -3 to 3
- inv_volume: float32 [16, 256, 1024], P(None, 'blocks', 'span'), may hold values from 0.04 to 0.16
- coord_cot: float32 [3, 16, 256, 1024], P(None, None, 'blocks', 'span'), may hold values from -6 to 6
- vol_cot: float32 [16, 256, 1024], P(None, 'blocks', 'span'), may hold values from -6 to 6
Outputs:
- warp_field: float32 [3, 16, 256, 1024], P(None, None, 'blocks', 'span')
- mesh_adjoint: float32 [3, 16, 256, 1024], P(None, None, 'blocks', 'span')
- struct_sens: float32 [3, 16384], P(None, ('blocks', 'span'))
Inputs may be any that keep to these rules, and one draw needn't show every extreme that they name: `rec_block`: in the rows of one device no fluid group is named by more than 128 records, and on some devices one group is named by exactly 128.
All inputs are finite; a program needn't handle non-finite values.
Results may differ from a plain program's by a relative error of at most 0.00002.
Values sent between devices are 32-bit elements; how exact they have to be, the bound alone decides.
A program may use at most 128 MiB of HBM per device.

v0:
```python
import functools

import jax
import jax.numpy as jnp
from jax import lax
from jax.experimental import pallas as pl
from jax.experimental.pallas import tpu as pltpu
from jax.sharding import PartitionSpec as P

SWEEPS = 4
LANES = 128
SUB = 8
MESH = pl.DeviceIdType.MESH


def split3(x):
    hi = x.astype(jnp.bfloat16)
    rest = x - hi.astype(jnp.float32)
    mid = rest.astype(jnp.bfloat16)
    low = (rest - mid.astype(jnp.float32)).astype(jnp.bfloat16)
    return hi, mid, low


def iota(shape, dim):
    return lax.broadcasted_iota(jnp.int32, shape, dim)


def kernel(
    groups,
    slabs,
    rec,
    disp,
    offset,
    prior,
    inv,
    cot,
    vol,
    warp_o,
    adj_o,
    sens_o,
    va,
    vb,
    sb,
    low_i,
    rec_send,
    rec_got,
    reply_send,
    reply_got,
    ja_send,
    ja_got,
    ka_send,
    ka_got,
    ca_got,
    surf_got,
    jb_send,
    jb_got,
    kb_send,
    kb_got,
    cb_got,
    jc_send,
    jc_got,
    kc_send,
    kc_got,
    cc_got,
    sem_rec,
    sem_reply,
    sem_halo,
):
    ni, nj, nk = offset.shape[1:]
    half = ni // 2
    np_j, np_k = nj + SUB, nk + LANES
    records = rec.shape[1]
    f32, bf16 = jnp.float32, jnp.bfloat16
    me = lax.axis_index("blocks")
    my = lax.axis_index("span")
    has = (me > 0, me < groups - 1, my > 0, my < slabs - 1)
    where_to = ((me - 1, my), (me + 1, my), (me, my - 1), (me, my + 1))

    barrier = pltpu.get_barrier_semaphore()
    for step in range(1, groups):
        pl.semaphore_signal(
            barrier, inc=1, device_id=(lax.rem(me + step, groups), my), device_id_type=MESH
        )
    for side in (2, 3):

        @pl.when(has[side])
        def _(side=side):
            pl.semaphore_signal(barrier, inc=1, device_id=where_to[side], device_id_type=MESH)

    struct_row = rec[0:1, :]
    onehot_s = (iota((disp.shape[1], records), 0).astype(f32) == struct_row).astype(bf16)
    parts = jnp.concatenate(split3(disp[...]), axis=0)
    gathered = jnp.dot(parts, onehot_s, preferred_element_type=f32)
    moved = (gathered[0:3] + gathered[3:6] + gathered[6:9]) * rec[3:4, :]
    rec_send[0:3, :] = moved
    rec_send[3:5, :] = rec[1:3, :]
    rec_send[5:8, :] = jnp.zeros((3, records), f32)

    pl.semaphore_wait(
        barrier, groups - 1 + has[2].astype(jnp.int32) + has[3].astype(jnp.int32)
    )

    def rec_copy(step):
        return pltpu.make_async_remote_copy(
            src_ref=rec_send,
            dst_ref=rec_got.at[me],
            send_sem=sem_rec.at[0, step],
            recv_sem=sem_rec.at[1, step],
            device_id=(lax.rem(me + step, groups), my),
            device_id_type=MESH,
        )

    for step in range(1, groups):
        rec_copy(step).start()
    rec_got[me] = rec_send[...]

    def move(side, src, dst, number):
        return pltpu.make_async_remote_copy(
            src_ref=src,
            dst_ref=dst,
            send_sem=sem_halo.at[0, number, side],
            recv_sem=sem_halo.at[1, number, side],
            device_id=where_to[side],
            device_id_type=MESH,
        )

    def start(side, src, dst, number):
        @pl.when(has[side])
        def _():
            move(side, src, dst, number).start()

    def finish_recv(side, src, dst, number):
        @pl.when(has[side ^ 1])
        def _():
            move(side, src, dst, number).wait_recv()

    def finish_send(side, src, dst, number):
        @pl.when(has[side])
        def _():
            move(side, src, dst, number).wait_send()

    def clear_missing(side, ref):
        @pl.when(jnp.logical_not(has[side ^ 1]))
        def _():
            ref[...] = jnp.zeros(ref.shape, f32)

    row8 = iota((SUB, nk), 0)
    lane_nj = iota((nj, LANES), 1)
    lane_np = iota((np_j, LANES), 1)
    row_c = iota((SUB, LANES), 0)

    def pack_rows4(source, send, comps):
        for c in range(comps):

            @pl.loop(0, half)
            def _(i):
                a, b = source(c, i, 0), source(c, i + half, 0)
                send[0, c, i] = jnp.where(row8 < SWEEPS, a, pltpu.roll(b, SWEEPS, 0))
                a, b = source(c, i, nj - SUB), source(c, i + half, nj - SUB)
                send[1, c, i] = jnp.where(row8 < SWEEPS, pltpu.roll(b, SWEEPS, 0), a)

    def unpack_rows4(got, comps, store):
        for c in range(comps):

            @pl.loop(0, half)
            def _(i):
                after, before = got[0, c, i], got[1, c, i]
                store(c, i, jnp.where(row8 < SWEEPS, after, before))
                store(
                    c, i + half, pltpu.roll(jnp.where(row8 < SWEEPS, before, after), SWEEPS, 0)
                )

    def pack_lanes(source, send, comps, width):
        per = LANES // width
        total = comps * ni
        chunk = lane_nj // width
        for g in range(-(-total // per)):

            def step(p, kept, g=g):
                first, last = kept
                s = g * per + p
                c, i = s // ni, s % ni
                left = source[c, i, 0:nj, 0:LANES]
                right = source[c, i, 0:nj, nk - LANES : nk]
                both = pltpu.roll(
                    jnp.where(lane_nj < LANES // 2, left, right), p * width, 1
                )
                first = jnp.where(chunk == p, both, first)
                last = jnp.where(chunk == lax.rem(p + per - 1, per), both, last)
                return first, last

            zero = jnp.zeros((nj, LANES), f32)
            first, last = lax.fori_loop(
                0, min(per, total - g * per), step, (zero, zero), unroll=4
            )
            send[0, g] = first
            send[1, g] = last

    def unpack_lanes(got, target, comps, width):
        per = LANES // width
        total = comps * ni
        chunk = lane_np // width
        for g in range(-(-total // per)):
            after, before = got[0, g], got[1, g]

            def step(p, kept, g=g, after=after, before=before):
                s = g * per + p
                c, i = s // ni, s % ni
                both = jnp.where(chunk == p, after, before)
                target[c, i, :, nk:np_k] = pltpu.roll(
                    both, lax.rem(LANES - p * width, LANES), 1
                )
                return kept

            lax.fori_loop(0, min(per, total - g * per), step, 0, unroll=4)

    class Exchange:
        def __init__(self, number, j_send, j_got, k_send, k_got, c_got):
            self.j = [(j_send.at[s], j_got.at[s], number) for s in (0, 1)]
            self.k = [(k_send.at[s], k_got.at[s, :, 0:nj, :], number) for s in (0, 1)]
            self.c = [
                (
                    k_got.at[:, :, s * (nj - SUB) : s * (nj - SUB) + SUB, :],
                    c_got.at[s],
                    number + 1,
                )
                for s in (0, 1)
            ]
            self.k_got, self.c_got = k_got, c_got
            for s in (0, 1):
                clear_missing(s, j_got.at[s])
                clear_missing(2 + s, k_got.at[s, :, 0:nj, :])
                clear_missing(s, c_got.at[s])

        def start_j(self):
            for s in (0, 1):
                start(s, *self.j[s])

        def start_k(self):
            for s in (0, 1):
                start(2 + s, *self.k[s])

        def corners(self):
            for s in (0, 1):
                finish_recv(2 + s, *self.k[s])
            for s in (0, 1):
                start(s, *self.c[s])

        def finish(self):
            for s in (0, 1):
                finish_recv(s, *self.j[s])
                finish_recv(s, *self.c[s])
            for d in (0, 1):
                for g in range(self.k_got.shape[1]):
                    self.k_got[d, g, nj:np_j] = jnp.where(
                        row_c < SWEEPS, self.c_got[0, d, g], self.c_got[1, d, g]
                    )

        def sent(self):
            for s in (0, 1):
                finish_send(s, *self.j[s])
                finish_send(2 + s, *self.k[s])
                finish_send(s, *self.c[s])

    halo_a = Exchange(0, ja_send, ja_got, ka_send, ka_got, ca_got)

    def source_a(c, i, at):
        if c < 3:
            return prior[c, i, at : at + SUB, :]
        return inv[i, at : at + SUB, :]

    pack_rows4(source_a, ja_send, 4)
    halo_a.start_j()

    @pl.loop(0, ni)
    def _(i):
        for c in range(3):
            va[c, i, 0:nj, 0:nk] = prior[c, i]
        va[3, i, 0:nj, 0:nk] = inv[i]

    pack_lanes(va, ka_send, 4, SWEEPS)
    halo_a.start_k()

    row_p = iota((np_j, records), 0)
    row_of = (me * nj + jnp.where(row_p < nj + SWEEPS, row_p, row_p - np_j)).astype(f32)
    col_of = iota((nk, records), 0).astype(f32)

    for step in range(1, groups):
        rec_copy(step).wait_recv()

    def scatter(g, total):
        got = rec_got[g]
        here = row_of == got[3:4, :]
        cols = (col_of == got[4:5, :]).astype(bf16)
        pieces = split3(got[0:3, :])
        left = jnp.concatenate(
            [
                jnp.where(here, pieces[n][c : c + 1, :].astype(f32), 0.0)
                for n in range(3)
                for c in range(3)
            ],
            axis=0,
        ).astype(bf16)
        out = lax.dot_general(
            left, cols, (((1,), (1,)), ((), ())), preferred_element_type=f32
        )
        rows = 3 * np_j
        return total + (out[0:rows] + out[rows : 2 * rows] + out[2 * rows :])

    surface = lax.fori_loop(0, groups, scatter, jnp.zeros((3 * np_j, nk), f32))
    for c in range(3):
        va[c, 0, :, 0:nk] = surface[c * np_j : (c + 1) * np_j]

    halo_a.corners()
    surf = [
        (va.at[0:3, 0, :, s * (nk - LANES) : s * (nk - LANES) + LANES], surf_got.at[s], 6)
        for s in (0, 1)
    ]
    for s in (0, 1):
        clear_missing(2 + s, surf_got.at[s])
        start(2 + s, *surf[s])
    halo_a.finish()

    def store_a(c, i, tile):
        if c < 3:

            @pl.when(i > 0)
            def _():
                va[c, i, nj:np_j, 0:nk] = tile
        else:
            va[c, i, nj:np_j, 0:nk] = tile

    unpack_rows4(ja_got, 4, store_a)
    unpack_lanes(ka_got, va, 4, SWEEPS)
    for s in (0, 1):
        finish_recv(2 + s, *surf[s])
    for c in range(3):
        va[c, 0, :, nk:np_k] = jnp.where(
            lane_np < LANES // 2, surf_got[0, c], surf_got[1, c]
        )
    halo_a.sent()
    for s in (0, 1):
        finish_send(2 + s, *surf[s])

    for c in range(3):
        vb[c, 0] = va[c, 0]
        vb[c, ni - 1] = va[c, ni - 1]

    def around(x):
        return (
            pltpu.roll(x, 1, 0)
            + pltpu.roll(x, np_j - 1, 0)
            + pltpu.roll(x, 1, 1)
            + pltpu.roll(x, np_k - 1, 1)
        )

    for sweep in range(SWEEPS):
        src, dst = (va, vb) if sweep % 2 == 0 else (vb, va)

        @pl.loop(1, ni - 1)
        def _(i, src=src, dst=dst):
            rate = va[3, i]
            for c in range(3):
                x = src[c, i]
                total = around(x) + src[c, i + 1] + src[c, i - 1]
                dst[c, i] = x + rate * (total - 6.0 * x)

    done = va if SWEEPS % 2 == 0 else vb

    halo_b = Exchange(2, jb_send, jb_got, kb_send, kb_got, cb_got)

    @pl.loop(0, ni)
    def _(i):
        for c in range(3):
            own = done[c, i, 0:nj, 0:nk]
            warp_o[c, i] = own
            own = own + offset[c, i]
            sb[c, i, 0:nj, 0:nk] = own
            jb_send[0, c, pl.ds(i, 1)] = own[0:1]
            jb_send[1, c, pl.ds(i, 1)] = own[nj - 1 : nj]
        own = vol[i]
        sb[3, i, 0:nj, 0:nk] = own
        jb_send[0, 3, pl.ds(i, 1)] = own[0:1]
        jb_send[1, 3, pl.ds(i, 1)] = own[nj - 1 : nj]

    halo_b.start_j()
    pack_lanes(sb, kb_send, 4, 1)
    halo_b.start_k()
    halo_b.corners()
    halo_b.finish()

    @pl.loop(0, ni)
    def _(i):
        for c in range(4):
            after = jnp.broadcast_to(jb_got[0, c, pl.ds(i, 1)], (SUB, nk))
            before = jnp.broadcast_to(jb_got[1, c, pl.ds(i, 1)], (SUB, nk))
            sb[c, i, nj:np_j, 0:nk] = jnp.where(row8 < SWEEPS, after, before)

    unpack_lanes(kb_got, sb, 4, 1)
    halo_b.sent()

    row = iota((np_j, np_k), 0)
    lane = iota((np_j, np_k), 1)
    row_at = me * nj + jnp.where(row < nj + SWEEPS, row, row - np_j)
    lane_at = my * nk + jnp.where(lane < nk + LANES // 2, lane, lane - np_k)
    inside = (
        (row_at >= 0)
        & (row_at < groups * nj - 1)
        & (lane_at >= 0)
        & (lane_at < slabs * nk - 1)
    )

    def cross(a, b):
        return (
            a[1] * b[2] - a[2] * b[1],
            a[2] * b[0] - a[0] * b[2],
            a[0] * b[1] - a[1] * b[0],
        )

    low_i[...] = jnp.zeros(low_i.shape, f32)

    @pl.loop(0, ni)
    def _(i):
        above = jnp.minimum(i + 1, ni - 1)
        base = [sb[c, i] for c in range(3)]
        edge_i = [sb[c, above] - base[c] for c in range(3)]
        edge_j = [pltpu.roll(base[c], np_j - 1, 0) - base[c] for c in range(3)]
        edge_k = [pltpu.roll(base[c], np_k - 1, 1) - base[c] for c in range(3)]
        edge_i[0] = edge_i[0] + 1.0
        edge_j[1] = edge_j[1] + 1.0
        edge_k[2] = edge_k[2] + 1.0
        weight = jnp.where(inside & (i < ni - 1), sb[3, i], 0.0)
        grad_i = cross(edge_j, edge_k)
        grad_j = cross(edge_k, edge_i)
        grad_k = cross(edge_i, edge_j)
        rate = va[3, i, 0:nj, 0:nk]
        rate = jnp.where((i > 0) & (i < ni - 1), rate, 0.0)
        for c in range(3):
            gi = (weight * grad_i[c])[0:nj, 0:nk]
            gj = weight * grad_j[c]
            gk = weight * grad_k[c]
            rest = (pltpu.roll(gj, 1, 0) - gj) + (pltpu.roll(gk, 1, 1) - gk)
            out = cot[c, i] - gi + low_i[c] + rest[0:nj, 0:nk]
            low_i[c] = gi
            adj_o[c, i] = out
            va[c, i, 0:nj, 0:nk] = rate * out

    halo_c = Exchange(4, jc_send, jc_got, kc_send, kc_got, cc_got)

    def source_c(c, i, at):
        return va[c, i, at : at + SUB, 0:nk]

    pack_rows4(source_c, jc_send, 3)
    halo_c.start_j()
    pack_lanes(va, kc_send, 3, SWEEPS)
    halo_c.start_k()
    halo_c.corners()
    halo_c.finish()

    def store_c(c, i, tile):
        va[c, i, nj:np_j, 0:nk] = tile

    unpack_rows4(jc_got, 3, store_c)
    unpack_lanes(kc_got, va, 3, SWEEPS)
    halo_c.sent()
    for c in range(3):
        vb[c, 0] = jnp.zeros((np_j, np_k), f32)
        vb[c, ni - 1] = jnp.zeros((np_j, np_k), f32)

    for sweep in range(SWEEPS):
        src, dst = (va, vb) if sweep % 2 == 0 else (vb, va)

        for c in range(3):
            adj_o[c, 0] += src[c, 1, 0:nj, 0:nk]
            adj_o[c, ni - 1] += src[c, ni - 2, 0:nj, 0:nk]

        @pl.loop(1, ni - 1)
        def _(i, src=src, dst=dst, sweep=sweep):
            rate = va[3, i]
            for c in range(3):
                x = src[c, i]
                change = (around(x) + src[c, i + 1] + src[c, i - 1]) - 6.0 * x
                adj_o[c, i] += change[0:nj, 0:nk]
                if sweep < SWEEPS - 1:
                    dst[c, i] = x + rate * change

    wall = jnp.concatenate(
        [jnp.concatenate(split3(adj_o[c, 0]), axis=0) for c in range(3)], axis=0
    )
    row_w = (me * nj + iota((nj, records), 0)).astype(f32)

    def reply_copy(step):
        to = lax.rem(me + step, groups)
        return pltpu.make_async_remote_copy(
            src_ref=reply_send.at[to],
            dst_ref=reply_got.at[me],
            send_sem=sem_reply.at[0, step],
            recv_sem=sem_reply.at[1, step],
            device_id=(to, my),
            device_id_type=MESH,
        )

    @pl.loop(0, groups)
    def _(g):
        got = rec_got[g]
        cols = (col_of == got[4:5, :]).astype(bf16)
        here = row_w == got[3:4, :]
        out = jnp.dot(wall, cols, preferred_element_type=f32)
        for c in range(3):
            at = 3 * c * nj
            value = (
                out[at : at + nj] + out[at + nj : at + 2 * nj] + out[at + 2 * nj : at + 3 * nj]
            )
            reply_send[g, c : c + 1, :] = jnp.sum(
                jnp.where(here, value, 0.0), axis=0, keepdims=True
            )
        reply_send[g, 3:8, :] = jnp.zeros((5, records), f32)

    for step in range(1, groups):
        reply_copy(step).start()
    reply_got[me] = reply_send[me]
    for step in range(1, groups):
        reply_copy(step).wait_recv()
    total = lax.fori_loop(
        0, groups, lambda g, kept: kept + reply_got[g], jnp.zeros((SUB, records), f32)
    )
    weighted = jnp.concatenate(split3(total[0:3] * rec[3:4, :]), axis=0)
    onehot_s = (iota((disp.shape[1], records), 0).astype(f32) == rec[0:1, :]).astype(bf16)
    out = lax.dot_general(
        weighted, onehot_s, (((1,), (1,)), ((), ())), preferred_element_type=f32
    )
    sens_o[...] = out[0:3] + out[3:6] + out[6:9]
    for step in range(1, groups):
        reply_copy(step).wait_send()
        rec_copy(step).wait_send()


def body(
    struct_disp,
    rec_struct,
    rec_block,
    rec_node,
    rec_weight,
    offset,
    prior_warp,
    inv_volume,
    coord_cot,
    vol_cot,
):
    groups = lax.axis_size("blocks")
    slabs = lax.axis_size("span")
    _, ni, nj, nk = offset.shape
    records = rec_struct.shape[0]
    f32 = jnp.float32
    chord_row = rec_block[:, 0] * nj + rec_node // nk
    rec = jnp.stack(
        [
            rec_struct.astype(f32),
            chord_row.astype(f32),
            (rec_node % nk).astype(f32),
            rec_weight,
        ]
    )
    np_j, np_k = nj + SUB, nk + LANES
    half = ni // 2

    def halo_rows4(comps):
        return [pltpu.VMEM((2, comps, half, SUB, nk), f32)] * 2

    def halo_lanes(comps, width):
        count = -(-comps * ni * width // LANES)
        return [
            pltpu.VMEM((2, count, nj, LANES), f32),
            pltpu.VMEM((2, count, np_j, LANES), f32),
            pltpu.VMEM((2, 2, count, SUB, LANES), f32),
        ]

    vmem = pl.BlockSpec(memory_space=pltpu.VMEM)
    return pl.pallas_call(
        functools.partial(kernel, groups, slabs),
        out_shape=(
            jax.ShapeDtypeStruct(offset.shape, f32),
            jax.ShapeDtypeStruct(offset.shape, f32),
            jax.ShapeDtypeStruct(struct_disp.shape, f32),
        ),
        in_specs=[vmem] * 7,
        out_specs=[vmem] * 3,
        scratch_shapes=[
            pltpu.VMEM((4, ni, np_j, np_k), f32),
            pltpu.VMEM((3, ni, np_j, np_k), f32),
            pltpu.VMEM((4, ni, np_j, np_k), f32),
            pltpu.VMEM((3, nj, nk), f32),
            pltpu.VMEM((SUB, records), f32),
            pltpu.VMEM((groups, SUB, records), f32),
            pltpu.VMEM((groups, SUB, records), f32),
            pltpu.VMEM((groups, SUB, records), f32),
            *halo_rows4(4),
            *halo_lanes(4, SWEEPS),
            pltpu.VMEM((2, 3, np_j, LANES), f32),
            *([pltpu.VMEM((2, 4, ni, nk), f32)] * 2),
            *halo_lanes(4, 1),
            *halo_rows4(3),
            *halo_lanes(3, SWEEPS),
            pltpu.SemaphoreType.DMA((2, groups)),
            pltpu.SemaphoreType.DMA((2, groups)),
            pltpu.SemaphoreType.DMA((2, 7, 4)),
        ],
        compiler_params=pltpu.CompilerParams(
            collective_id=0, has_side_effects=True, vmem_limit_bytes=60 * 1024 * 1024
        ),
        name="warp_adjoint",
    )(rec, struct_disp, offset, prior_warp, inv_volume, coord_cot, vol_cot)


def solution(mesh):
    placed = (
        P(None, ("blocks", "span")),
        P(("blocks", "span")),
        P(("blocks", "span"), None),
        P(("blocks", "span")),
        P(("blocks", "span")),
        P(None, None, "blocks", "span"),
        P(None, None, "blocks", "span"),
        P(None, "blocks", "span"),
        P(None, None, "blocks", "span"),
        P(None, "blocks", "span"),
    )
    return jax.shard_map(
        body,
        mesh=mesh,
        in_specs=placed,
        out_specs=(
            P(None, None, "blocks", "span"),
            P(None, None, "blocks", "span"),
            P(None, ("blocks", "span")),
        ),
        check_vma=False,
    )
```

profile of v0, /device:TPU:3, one launch (start us, length us, event | category | flops | bytes accessed | tf_op | source)
XLA Modules:
  0.0 85.3 jit_solution(4368877492912004763)
XLA Ops:
  0.6 0.7 convert_element_type.9
  1.3 0.7 broadcast_multiply_fusion
  2.0 0.7 fusion.1
  2.7 1.3 %pad_maximum_fusion.rec = f32[4,512]{1,0:T(4,128)} fusion(f32[1,512]{1,0:T(1,128)} %bitcast.9, f32[1,512]{1,0:T(1,128)S(1)} %bitcast.8, f32[1,512]{1,0:T(1,128)S(1)} %bitcast.7, f32[1,512]{1,0:T(1,128)S(1)} %bitcast.6), kind=kLoop, calls=%fused_computation | loop fusion | flops 6144 | bytes 16384 | tf_op jit(solution)/shard_map/stack | solution.py:556
  4.0 76.8 %warp_adjoint.1 = (f32[3,16,32,256]{3,2,1,0:T(8,128)}, f32[3,16,32,256]{3,2,1,0:T(8,128)}, f32[3,512]{1,0:T(4,128)}) custom-call(f32[4,512]{1,0:T(4,128)} %pad_maximum_fusion.rec, f32[3,512]{1,0:T(4,128)} %disp.1, f32[3,16,32,256]{3,2,1,0:T(8,128)} %offset.1, f32[3,16,32,256]{3,2,1,0:T(8,128)} %prior.1, f32[16,32,256]{2,1,0:T(8,128)} %inv.1, ...), custom_call_target="tpu_custom_call" | custom-call | tf_op jit(solution)/shard_map/warp_adjoint/pallas_call | solution.py:579
  80.7 0.0 copy-start
  80.8 2.8 %copy.16 = f32[3,16,32,256]{3,2,1,0:T(8,128)} copy(f32[3,16,32,256]{3,2,1,0:T(8,128)} %get-tuple-element.8) | data formatting | bytes 3145728
  83.6 0.0 copy-done
  83.6 0.0 copy-start.1
  83.6 1.1 %copy.17 = f32[3,16,32,256]{3,2,1,0:T(8,128)} copy(f32[3,16,32,256]{3,2,1,0:T(8,128)S(1)} %copy-done) | data formatting | bytes 3145728
  84.7 0.0 copy-done.1
  84.7 0.6 copy.18
Async XLA Ops:
  80.7 2.9 %copy-start = (f32[3,16,32,256]{3,2,1,0:T(8,128)S(1)}, f32[3,16,32,256]{3,2,1,0:T(8,128)}, u32[]{:S(2)}) copy-start(f32[3,16,32,256]{3,2,1,0:T(8,128)} %get-tuple-element.9) | copy-start | bytes 4718596
  83.6 1.1 %copy-start.1 = (f32[3,512]{1,0:T(4,128)S(1)}, f32[3,512]{1,0:T(4,128)}, u32[]{:S(2)}) copy-start(f32[3,512]{1,0:T(4,128)} %get-tuple-element.10) | copy-start | bytes 18436
where the time goes:
time: 86.6 us; the launch traced here: 85.3 us
  Pallas kernels  76.8 us (89%)
  local copies, waits for them, and re-layouts  4.59 us (5%)
  other arithmetic  3.35 us (4%)
    pallas_call x1, Pallas kernels, body(): pl.pallas_call(functools.partial(kernel, groups, slabs), out_shape=(jax.S...  76.8 us
    unnamed x7, local copies, waits for them, and re-layouts  4.59 us

commit v1 on v0

v1 whole, which is shorter than its diff:
```python
import functools

import jax
import jax.numpy as jnp
from jax import lax
from jax.experimental import pallas as pl
from jax.experimental.pallas import tpu as pltpu
from jax.sharding import PartitionSpec as P

SWEEPS = 4
LANES = 128
SUB = 8
VMEM_LIMIT = 44 * 1024 * 1024
MESH = pl.DeviceIdType.MESH


def split3(x):
    hi = x.astype(jnp.bfloat16)
    rest = x - hi.astype(jnp.float32)
    mid = rest.astype(jnp.bfloat16)
    low = (rest - mid.astype(jnp.float32)).astype(jnp.bfloat16)
    return hi, mid, low


def iota(shape, dim):
    return lax.broadcasted_iota(jnp.int32, shape, dim)


def kernel(
    groups,
    slabs,
    struct_of,
    block_of,
    node_of,
    weight_of,
    disp,
    offset,
    prior,
    inv,
    cot,
    vol,
    warp_o,
    adj_o,
    sens_o,
    va,
    vb,
    sb,
    low_i,
    low_j,
    rec_send,
    rec_got,
    reply_send,
    reply_got,
    ja_send,
    ja_got,
    ka_send,
    ka_got,
    surf_got,
    jb_send,
    jb_got,
    kb_send,
    kb_got,
    jc_send,
    jc_got,
    kc_send,
    kc_got,
    sem_rec,
    sem_reply,
    sem_halo,
):
    ni, nj, nk = offset.shape[1:]
    half = ni // 2
    np_j = nj + SUB
    tiles = nk // LANES
    own, top, end = slice(SUB, SUB + nj), slice(0, SUB), slice(SUB + nj, SUB + nj + SUB)
    near = SUB - SWEEPS
    records = struct_of.shape[0]
    f32, bf16 = jnp.float32, jnp.bfloat16
    me = lax.axis_index("blocks")
    my = lax.axis_index("span")
    has = (me > 0, me < groups - 1, my > 0, my < slabs - 1)
    where_to = ((me - 1, my), (me + 1, my), (me, my - 1), (me, my + 1))

    barrier = pltpu.get_barrier_semaphore()
    for step in range(1, groups):
        pl.semaphore_signal(
            barrier, inc=1, device_id=(lax.rem(me + step, groups), my), device_id_type=MESH
        )
    for side in (2, 3):

        @pl.when(has[side])
        def _(side=side):
            pl.semaphore_signal(barrier, inc=1, device_id=where_to[side], device_id_type=MESH)

    def flat(ref):
        return ref[...].reshape(1, records)

    weights = flat(weight_of)
    node = flat(node_of)
    row_in = node // nk
    onehot_s = (iota((disp.shape[1], records), 0) == flat(struct_of)).astype(bf16)
    parts = jnp.concatenate(split3(disp[...]), axis=0)
    gathered = jnp.dot(parts, onehot_s, preferred_element_type=f32)
    rec_send[0:3, :] = (gathered[0:3] + gathered[3:6] + gathered[6:9]) * weights
    rec_send[3:4, :] = (flat(block_of) * nj + row_in).astype(f32)
    rec_send[4:5, :] = (node - row_in * nk).astype(f32)
    rec_send[5:8, :] = jnp.zeros((3, records), f32)

    pl.semaphore_wait(
        barrier, groups - 1 + has[2].astype(jnp.int32) + has[3].astype(jnp.int32)
    )

    def rec_copy(step):
        return pltpu.make_async_remote_copy(
            src_ref=rec_send,
            dst_ref=rec_got.at[me],
            send_sem=sem_rec.at[0, step],
            recv_sem=sem_rec.at[1, step],
            device_id=(lax.rem(me + step, groups), my),
            device_id_type=MESH,
        )

    for step in range(1, groups):
        rec_copy(step).start()
    rec_got[me] = rec_send[...]

    def move(side, src, dst, number):
        return pltpu.make_async_remote_copy(
            src_ref=src,
            dst_ref=dst,
            send_sem=sem_halo.at[0, number, side],
            recv_sem=sem_halo.at[1, number, side],
            device_id=where_to[side],
            device_id_type=MESH,
        )

    def start(side, src, dst, number):
        @pl.when(has[side])
        def _():
            move(side, src, dst, number).start()

    def finish_recv(side, src, dst, number):
        @pl.when(has[side ^ 1])
        def _():
            move(side, src, dst, number).wait_recv()

    def finish_send(side, src, dst, number):
        @pl.when(has[side])
        def _():
            move(side, src, dst, number).wait_send()

    def clear_missing(side, ref):
        @pl.when(jnp.logical_not(has[side ^ 1]))
        def _():
            ref[...] = jnp.zeros(ref.shape, f32)

    row8 = iota((SUB, nk), 0)
    lane_nj = iota((nj, LANES), 1)
    rows_k = nj + 2 * SUB
    lane_np = iota((rows_k, LANES), 1)

    def pack_rows4(source, send, comps):
        for c in range(comps):

            @pl.loop(0, half)
            def _(i):
                a, b = source(c, i, 0), source(c, i + half, 0)
                send[0, c, i] = jnp.where(row8 < SWEEPS, a, pltpu.roll(b, SWEEPS, 0))
                a, b = source(c, i, nj - SUB), source(c, i + half, nj - SUB)
                send[1, c, i] = jnp.where(row8 < SWEEPS, pltpu.roll(b, SWEEPS, 0), a)

    def put(target, c, i, rows, value):
        for t in range(tiles):
            target[c, i, t, rows, :] = value[:, t * LANES : (t + 1) * LANES]

    def unpack_rows4(got, comps, store):
        for c in range(comps):

            @pl.loop(0, half)
            def _(i):
                for side, rows in ((0, end), (1, top)):
                    x = got[side, c, i]
                    store(c, i, rows, x)
                    store(c, i + half, rows, pltpu.roll(x, SWEEPS, 0))

    def pack_lanes(source, send, comps, width):
        per = LANES // width
        total = comps * ni
        chunk = lane_nj // width
        for g in range(-(-total // per)):

            def step(p, kept, g=g):
                first, last = kept
                s = g * per + p
                c, i = s // ni, s % ni
                left = source[c, i, 0, own, :]
                right = source[c, i, tiles - 1, own, :]
                both = pltpu.roll(
                    jnp.where(lane_nj < LANES // 2, left, right), p * width, 1
                )
                first = jnp.where(chunk == p, both, first)
                last = jnp.where(chunk == lax.rem(p + per - 1, per), both, last)
                return first, last

            zero = jnp.zeros((nj, LANES), f32)
            first, last = lax.fori_loop(
                0, min(per, total - g * per), step, (zero, zero), unroll=4
            )
            send[0, g] = first
            send[1, g] = last

    def unpack_lanes(got, target, comps, width):
        per = LANES // width
        total = comps * ni
        chunk = lane_np // width
        for g in range(-(-total // per)):
            after, before = got[0, g], got[1, g]

            def step(p, kept, g=g, after=after, before=before):
                s = g * per + p
                c, i = s // ni, s % ni
                both = jnp.where(chunk == p, after, before)
                target[c, i, tiles] = pltpu.roll(both, lax.rem(LANES - p * width, LANES), 1)
                return kept

            lax.fori_loop(0, min(per, total - g * per), step, 0, unroll=4)

    class Exchange:
        def __init__(self, number, j_send, j_got, k_send, k_got):
            self.j = [(j_send.at[s], j_got.at[s], number) for s in (0, 1)]
            self.k = [(k_send.at[s], k_got.at[s, :, own, :], number) for s in (0, 1)]
            self.c = []
            for s in (0, 1):
                at = SUB + s * (nj - SUB)
                to = (end, top)[s]
                self.c.append(
                    (k_got.at[:, :, at : at + SUB, :], k_got.at[:, :, to, :], number + 1)
                )
                clear_missing(s, j_got.at[s])
                clear_missing(2 + s, k_got.at[s, :, own, :])
                clear_missing(s, k_got.at[:, :, to, :])

        def start_j(self):
            for s in (0, 1):
                start(s, *self.j[s])

        def start_k(self):
            for s in (0, 1):
                start(2 + s, *self.k[s])

        def corners(self):
            for s in (0, 1):
                finish_recv(2 + s, *self.k[s])
            for s in (0, 1):
                start(s, *self.c[s])

        def finish(self):
            for s in (0, 1):
                finish_recv(s, *self.j[s])
                finish_recv(s, *self.c[s])

        def sent(self):
            for s in (0, 1):
                finish_send(s, *self.j[s])
                finish_send(2 + s, *self.k[s])
                finish_send(s, *self.c[s])

    halo_a = Exchange(0, ja_send, ja_got, ka_send, ka_got)

    def source_a(c, i, at):
        if c < 3:
            return prior[c, i, at : at + SUB, :]
        return inv[i, at : at + SUB, :]

    pack_rows4(source_a, ja_send, 4)
    halo_a.start_j()

    @pl.loop(0, ni)
    def _(i):
        for c in range(3):
            put(va, c, i, own, prior[c, i])
        put(va, 3, i, own, inv[i])

    pack_lanes(va, ka_send, 4, SWEEPS)
    halo_a.start_k()

    row_p = iota((np_j, records), 0)
    row_of = (me * nj + row_p - SWEEPS).astype(f32)
    col_of = iota((nk, records), 0).astype(f32)

    for step in range(1, groups):
        rec_copy(step).wait_recv()

    def scatter(g, total):
        got = rec_got[g]
        here = row_of == got[3:4, :]
        cols = (col_of == got[4:5, :]).astype(bf16)
        pieces = split3(got[0:3, :])
        left = jnp.concatenate(
            [
                jnp.where(here, pieces[n][c : c + 1, :].astype(f32), 0.0)
                for n in range(3)
                for c in range(3)
            ],
            axis=0,
        ).astype(bf16)
        out = lax.dot_general(
            left, cols, (((1,), (1,)), ((), ())), preferred_element_type=f32
        )
        rows = 3 * np_j
        return total + (out[0:rows] + out[rows : 2 * rows] + out[2 * rows :])

    surface = lax.fori_loop(0, groups, scatter, jnp.zeros((3 * np_j, nk), f32))
    for c in range(3):
        put(va, c, 0, slice(near, near + np_j), surface[c * np_j : (c + 1) * np_j])

    halo_a.corners()
    surf = [
        (va.at[0:3, 0, s * (tiles - 1)], surf_got.at[s], 6)
        for s in (0, 1)
    ]
    for s in (0, 1):
        clear_missing(2 + s, surf_got.at[s])
        start(2 + s, *surf[s])
    halo_a.finish()

    def store_a(c, i, rows, value):
        if c < 3:

            @pl.when(i > 0)
            def _():
                put(va, c, i, rows, value)
        else:
            put(va, c, i, rows, value)

    unpack_rows4(ja_got, 4, store_a)
    unpack_lanes(ka_got, va, 4, SWEEPS)
    for s in (0, 1):
        finish_recv(2 + s, *surf[s])
    for c in range(3):
        va[c, 0, tiles] = jnp.where(lane_np < LANES // 2, surf_got[0, c], surf_got[1, c])
    halo_a.sent()
    for s in (0, 1):
        finish_send(2 + s, *surf[s])

    for c in range(3):
        vb[c, 0] = va[c, 0]
        vb[c, ni - 1] = va[c, ni - 1]

    def nearby(rows):
        return slice(rows.start - 1, rows.stop - 1), slice(rows.start + 1, rows.stop + 1)

    def lane_before(x, rolled):
        lane = iota(x[0].shape, 1)
        return [jnp.where(lane == 0, rolled[t - 1], rolled[t]) for t in range(len(x))]

    def lane_after(x, rolled):
        lane = iota(x[0].shape, 1)
        count = len(x)
        return [
            jnp.where(lane == LANES - 1, rolled[(t + 1) % count], rolled[t])
            for t in range(count)
        ]

    def changes(src, c, i, rows, count):
        low, high = nearby(rows)
        x = [src[c, i, t, rows, :] for t in range(tiles + 1)]
        before = lane_before(x, [pltpu.roll(v, 1, 1) for v in x])
        after = lane_after(x, [pltpu.roll(v, LANES - 1, 1) for v in x])
        out = []
        for t in range(count):
            total = before[t] + after[t]
            total = total + (src[c, i, t, low, :] + src[c, i, t, high, :])
            total = total + (src[c, i - 1, t, rows, :] + src[c, i + 1, t, rows, :])
            out.append(total - 6.0 * x[t])
        return x, out

    wide = slice(near, near + np_j)

    def sweep_a(src, dst, last):
        rows, count = (own, tiles) if last else (wide, tiles + 1)

        @pl.loop(1, ni - 1)
        def _(i):
            for c in range(3):
                x, change = changes(src, c, i, rows, count)
                for t in range(count):
                    dst[c, i, t, rows, :] = x[t] + va[3, i, t, rows, :] * change[t]

    for sweep in range(SWEEPS):
        src, dst = (va, vb) if sweep % 2 == 0 else (vb, va)
        sweep_a(src, dst, sweep == SWEEPS - 1)

    done = va if SWEEPS % 2 == 0 else vb

    halo_b = Exchange(2, jb_send, jb_got, kb_send, kb_got)

    @pl.loop(0, ni)
    def _(i):
        for c in range(4):
            for t in range(tiles):
                lanes = slice(t * LANES, (t + 1) * LANES)
                if c < 3:
                    value = done[c, i, t, own, :]
                    warp_o[c, i, :, lanes] = value
                    value = value + offset[c, i, :, lanes]
                else:
                    value = vol[i, :, lanes]
                sb[c, i, t, own, :] = value
                jb_send[0, c, t, pl.ds(i, 1), :] = value[0:1]
                jb_send[1, c, t, pl.ds(i, 1), :] = value[nj - 1 : nj]

    halo_b.start_j()
    pack_lanes(sb, kb_send, 4, 1)
    halo_b.start_k()
    halo_b.corners()
    halo_b.finish()

    @pl.loop(0, ni)
    def _(i):
        for c in range(4):
            for side, rows in ((0, end), (1, top)):
                for t in range(tiles):
                    sb[c, i, t, rows, :] = jnp.broadcast_to(
                        jb_got[side, c, t, pl.ds(i, 1), :], (SUB, LANES)
                    )

    unpack_lanes(kb_got, sb, 4, 1)
    halo_b.sent()

    lane = iota((np_j, LANES), 1)
    row_at = me * nj + iota((np_j, LANES), 0) - SWEEPS
    row_in = (row_at >= 0) & (row_at < groups * nj - 1)

    def inside(t):
        if t < tiles:
            at = my * nk + t * LANES + lane
        else:
            at = my * nk + lane - LANES
        return row_in & (at >= 0) & (at < slabs * nk - 1)

    def cross(a, b):
        return (
            a[1] * b[2] - a[2] * b[1],
            a[2] * b[0] - a[0] * b[2],
            a[0] * b[1] - a[1] * b[0],
        )

    low_i[...] = jnp.zeros(low_i.shape, f32)
    mine = slice(SWEEPS, SWEEPS + nj)
    _, wide_high = nearby(wide)

    @pl.loop(0, ni)
    def _(i):
        above = jnp.minimum(i + 1, ni - 1)
        held = None
        for t in (tiles, *range(tiles)):
            follow = (t + 1) % (tiles + 1)
            base = [sb[c, i, t, wide, :] for c in range(3)]
            edge_i = [sb[c, above, t, wide, :] - base[c] for c in range(3)]
            edge_j = [sb[c, i, t, wide_high, :] - base[c] for c in range(3)]
            edge_k = [
                jnp.where(
                    lane == LANES - 1,
                    pltpu.roll(sb[c, i, follow, wide, :], LANES - 1, 1),
                    pltpu.roll(base[c], LANES - 1, 1),
                )
                - base[c]
                for c in range(3)
            ]
            edge_i[0] = edge_i[0] + 1.0
            edge_j[1] = edge_j[1] + 1.0
            edge_k[2] = edge_k[2] + 1.0
            weight = jnp.where(inside(t) & (i < ni - 1), sb[3, i, t, wide, :], 0.0)
            grad_k = [pltpu.roll(weight * g, 1, 1) for g in cross(edge_i, edge_j)]
            if t < tiles:
                grad_i = cross(edge_j, edge_k)
                grad_j = cross(edge_k, edge_i)
                rate = va[3, i, t, own, :]
                rate = jnp.where((i > 0) & (i < ni - 1), rate, 0.0)
                for c in range(3):
                    gi = (weight * grad_i[c])[mine]
                    low_j[c, t] = weight * grad_j[c]
                    gk = weight * cross(edge_i, edge_j)[c]
                    rest = jnp.where(lane == 0, held[c], grad_k[c]) - gk
                    rest = rest[mine] + (
                        low_j[c, t, SWEEPS - 1 : SWEEPS - 1 + nj, :] - low_j[c, t, mine, :]
                    )
                    lanes = slice(t * LANES, (t + 1) * LANES)
                    out = cot[c, i, :, lanes] - gi + low_i[c, t] + rest
                    low_i[c, t] = gi
                    adj_o[c, i, :, lanes] = out
                    va[c, i, t, own, :] = rate * out
            held = grad_k

    halo_c = Exchange(4, jc_send, jc_got, kc_send, kc_got)

    def source_c(c, i, at):
        return jnp.concatenate(
            [va[c, i, t, SUB + at : 2 * SUB + at, :] for t in range(tiles)], axis=1
        )

    pack_rows4(source_c, jc_send, 3)
    halo_c.start_j()
    pack_lanes(va, kc_send, 3, SWEEPS)
    halo_c.start_k()
    halo_c.corners()
    halo_c.finish()

    def store_c(c, i, rows, value):
        put(va, c, i, rows, value)

    unpack_rows4(jc_got, 3, store_c)
    unpack_lanes(kc_got, va, 3, SWEEPS)
    halo_c.sent()
    for c in range(3):
        vb[c, 0] = jnp.zeros(vb.shape[2:], f32)
        vb[c, ni - 1] = jnp.zeros(vb.shape[2:], f32)

    def sweep_c(sweep, first, stop):
        src, dst = (va, vb) if sweep % 2 == 0 else (vb, va)
        last = sweep == SWEEPS - 1
        rows, count = (own, tiles) if last else (wide, tiles + 1)
        kept = slice(0, nj) if last else mine

        @pl.loop(first, stop)
        def _(i):
            for c in range(3):
                x, change = changes(src, c, i, rows, count)
                for t in range(count):
                    if t < tiles:
                        adj_o[c, i, :, t * LANES : (t + 1) * LANES] += change[t][kept]
                    if not last:
                        dst[c, i, t, rows, :] = x[t] + va[3, i, t, rows, :] * change[t]

    def add_wall(sweep, wall, layer):
        src = va if sweep % 2 == 0 else vb
        for c in range(3):
            for t in range(tiles):
                adj_o[c, wall, :, t * LANES : (t + 1) * LANES] += src[c, layer, t, own, :]

    add_wall(0, 0, 1)
    for sweep in range(SWEEPS - 1):
        sweep_c(sweep, 1, SWEEPS - sweep)
        add_wall(sweep + 1, 0, 1)

    wall = jnp.concatenate(
        [jnp.concatenate(split3(adj_o[c, 0]), axis=0) for c in range(3)], axis=0
    )
    row_w = (me * nj + iota((nj, records), 0)).astype(f32)

    def reply_copy(step):
        to = lax.rem(me + step, groups)
        return pltpu.make_async_remote_copy(
            src_ref=reply_send.at[to],
            dst_ref=reply_got.at[me],
            send_sem=sem_reply.at[0, step],
            recv_sem=sem_reply.at[1, step],
            device_id=(to, my),
            device_id_type=MESH,
        )

    @pl.loop(0, groups)
    def _(g):
        got = rec_got[g]
        cols = (col_of == got[4:5, :]).astype(bf16)
        here = row_w == got[3:4, :]
        out = jnp.dot(wall, cols, preferred_element_type=f32)
        for c in range(3):
            at = 3 * c * nj
            value = (
                out[at : at + nj] + out[at + nj : at + 2 * nj] + out[at + 2 * nj : at + 3 * nj]
            )
            reply_send[g, c : c + 1, :] = jnp.sum(
                jnp.where(here, value, 0.0), axis=0, keepdims=True
            )
        reply_send[g, 3:8, :] = jnp.zeros((5, records), f32)

    for step in range(1, groups):
        reply_copy(step).start()
    reply_got[me] = reply_send[me]
    for sweep in range(SWEEPS):
        add_wall(sweep, ni - 1, ni - 2)
        sweep_c(sweep, SWEEPS - sweep if sweep < SWEEPS - 1 else 1, ni - 1)

    for step in range(1, groups):
        reply_copy(step).wait_recv()
    total = lax.fori_loop(
        0, groups, lambda g, kept: kept + reply_got[g], jnp.zeros((SUB, records), f32)
    )
    weighted = jnp.concatenate(split3(total[0:3] * weights), axis=0)
    out = lax.dot_general(
        weighted, onehot_s, (((1,), (1,)), ((), ())), preferred_element_type=f32
    )
    sens_o[...] = out[0:3] + out[3:6] + out[6:9]
    for step in range(1, groups):
        reply_copy(step).wait_send()
        rec_copy(step).wait_send()


def body(
    struct_disp,
    rec_struct,
    rec_block,
    rec_node,
    rec_weight,
    offset,
    prior_warp,
    inv_volume,
    coord_cot,
    vol_cot,
):
    groups = lax.axis_size("blocks")
    slabs = lax.axis_size("span")
    _, ni, nj, nk = offset.shape
    records = rec_struct.shape[0]
    f32 = jnp.float32
    rows_k = nj + 2 * SUB
    tiles = nk // LANES
    half = ni // 2

    def halo_rows4(comps):
        return [pltpu.VMEM((2, comps, half, SUB, nk), f32)] * 2

    def halo_lanes(comps, width):
        count = -(-comps * ni * width // LANES)
        return [
            pltpu.VMEM((2, count, nj, LANES), f32),
            pltpu.VMEM((2, count, rows_k, LANES), f32),
        ]

    vmem = pl.BlockSpec(memory_space=pltpu.VMEM)
    outs = pl.pallas_call(
        functools.partial(kernel, groups, slabs),
        out_shape=(
            jax.ShapeDtypeStruct(offset.shape, f32),
            jax.ShapeDtypeStruct(offset.shape, f32),
            jax.ShapeDtypeStruct(struct_disp.shape, f32),
        ),
        in_specs=[vmem] * 10,
        out_specs=[vmem] * 3,
        scratch_shapes=[
            pltpu.VMEM((4, ni, tiles + 1, rows_k, LANES), f32),
            pltpu.VMEM((3, ni, tiles + 1, rows_k, LANES), f32),
            pltpu.VMEM((4, ni, tiles + 1, rows_k, LANES), f32),
            pltpu.VMEM((3, tiles, nj, LANES), f32),
            pltpu.VMEM((3, tiles, nj + SUB, LANES), f32),
            pltpu.VMEM((SUB, records), f32),
            pltpu.VMEM((groups, SUB, records), f32),
            pltpu.VMEM((groups, SUB, records), f32),
            pltpu.VMEM((groups, SUB, records), f32),
            *halo_rows4(4),
            *halo_lanes(4, SWEEPS),
            pltpu.VMEM((2, 3, rows_k, LANES), f32),
            *([pltpu.VMEM((2, 4, tiles, ni, LANES), f32)] * 2),
            *halo_lanes(4, 1),
            *halo_rows4(3),
            *halo_lanes(3, SWEEPS),
            pltpu.SemaphoreType.DMA((2, groups)),
            pltpu.SemaphoreType.DMA((2, groups)),
            pltpu.SemaphoreType.DMA((2, 7, 4)),
        ],
        compiler_params=pltpu.CompilerParams(
            collective_id=0, has_side_effects=True, vmem_limit_bytes=VMEM_LIMIT
        ),
        name="warp_adjoint",
    )(
        rec_struct,
        rec_block.reshape(records),
        rec_node,
        rec_weight,
        struct_disp,
        offset,
        prior_warp,
        inv_volume,
        coord_cot,
        vol_cot,
    )
    return outs


def solution(mesh):
    placed = (
        P(None, ("blocks", "span")),
        P(("blocks", "span")),
        P(("blocks", "span"), None),
        P(("blocks", "span")),
        P(("blocks", "span")),
        P(None, None, "blocks", "span"),
        P(None, None, "blocks", "span"),
        P(None, "blocks", "span"),
        P(None, None, "blocks", "span"),
        P(None, "blocks", "span"),
    )
    return jax.shard_map(
        body,
        mesh=mesh,
        in_specs=placed,
        out_specs=(
            P(None, None, "blocks", "span"),
            P(None, None, "blocks", "span"),
            P(None, ("blocks", "span")),
        ),
        check_vma=False,
    )
```

time: 86.6 us -> 81.4 us (0.940)
  Pallas kernels: 76.8 us -> 67.7 us
  local copies, waits for them, and re-layouts: 4.59 us -> 12.6 us
  other arithmetic: 3.35 us -> 0 us
    pallas_call x1, Pallas kernels: 76.8 us -> 67.7 us  [body(): pl.pallas_call(functools.partial(kernel, groups, slabs), out_shape=(jax.S...]
    unnamed x7 -> x23, local copies, waits for them, and re-layouts: 4.59 us -> 12.6 us
    convert_element_type x2 -> x0, other arithmetic: 1.38 us -> none  [the longest x1 0.69 us: body(): chord_row.astype(f32)]
    another operation x1 -> x0, other arithmetic: 1.29 us -> none  [body(): jnp.stack([rec_struct.astype(f32), chord_row.astype(f32), (rec_node % nk)...]
where the time goes in v1:
time: 81.4 us; the launch traced here: 80.9 us
  Pallas kernels  67.7 us (83%)
  local copies, waits for them, and re-layouts  12.6 us (15%)
    pallas_call x1, Pallas kernels, body(): pl.pallas_call(functools.partial(kernel, groups, slabs), out_shape=(jax.S...  67.7 us
    unnamed x23, local copies, waits for them, and re-layouts  12.6 us

profile of v1, /device:TPU:3, one launch (start us, length us, event | category | flops | bytes accessed | tf_op | source)
XLA Modules:
  0.0 80.9 jit_solution(12555885546906451111)
XLA Ops:
  0.6 0.0 copy-start
  0.6 1.4 %copy-done = f32[3,16,32,256]{3,2,1,0:T(8,128)S(1)} copy-done((f32[3,16,32,256]{3,2,1,0:T(8,128)S(1)}, f32[3,16,32,256]{3,2,1,0:T(8,128)}, u32[]{:S(2)}) %copy-start) | copy-done | bytes 1572888
  2.0 0.0 copy-start.1
  2.0 1.4 %copy-done.1 = f32[3,16,32,256]{3,2,1,0:T(8,128)S(1)} copy-done((f32[3,16,32,256]{3,2,1,0:T(8,128)S(1)}, f32[3,16,32,256]{3,2,1,0:T(8,128)}, u32[]{:S(2)}) %copy-start.1) | copy-done | bytes 1572888
  3.5 0.0 copy-start.2
  3.5 1.4 %copy-done.2 = f32[3,16,32,256]{3,2,1,0:T(8,128)S(1)} copy-done((f32[3,16,32,256]{3,2,1,0:T(8,128)S(1)}, f32[3,16,32,256]{3,2,1,0:T(8,128)}, u32[]{:S(2)}) %copy-start.2) | copy-done | bytes 1572888
  4.9 0.0 copy-start.3
  4.9 1.0 %copy-done.3 = f32[16,32,256]{2,1,0:T(8,128)S(1)} copy-done((f32[16,32,256]{2,1,0:T(8,128)S(1)}, f32[16,32,256]{2,1,0:T(8,128)}, u32[]{:S(2)}) %copy-start.3) | copy-done | bytes 524312
  5.9 0.0 copy-start.4
  5.9 1.0 %copy-done.4 = f32[16,32,256]{2,1,0:T(8,128)S(1)} copy-done((f32[16,32,256]{2,1,0:T(8,128)S(1)}, f32[16,32,256]{2,1,0:T(8,128)}, u32[]{:S(2)}) %copy-start.4) | copy-done | bytes 524312
  6.9 0.0 copy-start.5
  6.9 0.7 copy-done.5
  7.6 0.0 copy-start.6
  7.6 0.7 copy-done.6
  8.3 0.0 copy-start.7
  8.3 0.7 copy-done.7
  9.0 0.0 copy-start.8
  9.0 0.7 copy-done.8
  9.7 0.0 copy-start.9
  9.7 0.7 copy-done.9
  10.4 67.7 %warp_adjoint.1 = (f32[3,16,32,256]{3,2,1,0:T(8,128)S(1)}, f32[3,16,32,256]{3,2,1,0:T(8,128)S(1)}, f32[3,512]{1,0:T(4,128)S(1)}) custom-call(s32[512]{0:T(512)S(1)} %copy-done.6, s32[512]{0:T(512)S(1)} %bitcast.1, s32[512]{0:T(512)S(1)} %copy-done.8, f32[512]{0:T(512)S(1)} %copy-done.9, f32[3,512]{1,0:T(4,128)S(1)} %copy-done.5, ...), custom_call_target="tpu_custom_call" | custom-call | tf_op jit(solution)/shard_map/warp_adjoint/pallas_call | solution.py:633
  78.0 1.1 %copy.16 = f32[3,16,32,256]{3,2,1,0:T(8,128)} copy(f32[3,16,32,256]{3,2,1,0:T(8,128)S(1)} %get-tuple-element.6) | data formatting | bytes 3145728
  79.2 1.1 %copy.17 = f32[3,16,32,256]{3,2,1,0:T(8,128)} copy(f32[3,16,32,256]{3,2,1,0:T(8,128)S(1)} %get-tuple-element.7) | data formatting | bytes 3145728
  80.3 0.6 copy.18
Async XLA Ops:
  0.6 1.4 %copy-start = (f32[3,16,32,256]{3,2,1,0:T(8,128)S(1)}, f32[3,16,32,256]{3,2,1,0:T(8,128)}, u32[]{:S(2)}) copy-start(f32[3,16,32,256]{3,2,1,0:T(8,128)} %offset.1) | copy-start | bytes 4718596
  2.0 1.4 %copy-start.1 = (f32[3,16,32,256]{3,2,1,0:T(8,128)S(1)}, f32[3,16,32,256]{3,2,1,0:T(8,128)}, u32[]{:S(2)}) copy-start(f32[3,16,32,256]{3,2,1,0:T(8,128)} %prior.1) | copy-start | bytes 4718596
  3.5 1.4 %copy-start.2 = (f32[3,16,32,256]{3,2,1,0:T(8,128)S(1)}, f32[3,16,32,256]{3,2,1,0:T(8,128)}, u32[]{:S(2)}) copy-start(f32[3,16,32,256]{3,2,1,0:T(8,128)} %cot.1) | copy-start | bytes 4718596
  4.9 1.0 %copy-start.3 = (f32[16,32,256]{2,1,0:T(8,128)S(1)}, f32[16,32,256]{2,1,0:T(8,128)}, u32[]{:S(2)}) copy-start(f32[16,32,256]{2,1,0:T(8,128)} %inv.1) | copy-start | bytes 1572868
  5.9 1.0 %copy-start.4 = (f32[16,32,256]{2,1,0:T(8,128)S(1)}, f32[16,32,256]{2,1,0:T(8,128)}, u32[]{:S(2)}) copy-start(f32[16,32,256]{2,1,0:T(8,128)} %vol.1) | copy-start | bytes 1572868
  6.9 0.7 copy-start.5
  7.6 0.7 copy-start.6
  8.3 0.7 copy-start.7
  9.0 0.7 copy-start.8
  9.7 0.7 copy-start.9

commit v2 on v1

--- a/solution.py
+++ b/solution.py
@@ -10,7 +10,7 @@
 SWEEPS = 4
 LANES = 128
 SUB = 8
-VMEM_LIMIT = 44 * 1024 * 1024
+VMEM_LIMIT = 62 * 1024 * 1024
 MESH = pl.DeviceIdType.MESH
 
 
@@ -34,12 +34,12 @@
     node_of,
     weight_of,
     disp,
-    offset,
-    prior,
-    inv,
-    cot,
-    vol,
-    warp_o,
+    offset_h,
+    prior_h,
+    inv_h,
+    cot_h,
+    vol_h,
+    warp_h,
     adj_o,
     sens_o,
     va,
@@ -67,19 +67,43 @@
     sem_rec,
     sem_reply,
     sem_halo,
+    cot,
+    sem_in,
+    sem_out,
 ):
-    ni, nj, nk = offset.shape[1:]
+    ni, nj, nk = offset_h.shape[1:]
     half = ni // 2
     np_j = nj + SUB
     tiles = nk // LANES
     own, top, end = slice(SUB, SUB + nj), slice(0, SUB), slice(SUB + nj, SUB + nj + SUB)
     near = SUB - SWEEPS
+    lanes_of = lambda t: slice(t * LANES, (t + 1) * LANES)
     records = struct_of.shape[0]
     f32, bf16 = jnp.float32, jnp.bfloat16
     me = lax.axis_index("blocks")
     my = lax.axis_index("span")
     has = (me > 0, me < groups - 1, my > 0, my < slabs - 1)
     where_to = ((me - 1, my), (me + 1, my), (me, my - 1), (me, my + 1))
+
+    def load(number, src, dst):
+        copies = []
+        for t in range(tiles):
+            lanes = slice(t * LANES, (t + 1) * LANES)
+            copies.append(
+                pltpu.make_async_copy(src(lanes), dst(t), sem_in.at[number, t])
+            )
+            copies[-1].start()
+        return copies
+
+    load_prior = load(0, lambda x: prior_h.at[:, :, :, x], lambda t: va.at[0:3, :, t, own, :])
+    load_inv = load(1, lambda x: inv_h.at[:, :, x], lambda t: va.at[3, :, t, own, :])
+    load_offset = load(2, lambda x: offset_h.at[:, :, :, x], lambda t: sb.at[0:3, :, t, own, :])
+    load_vol = load(3, lambda x: vol_h.at[:, :, x], lambda t: sb.at[3, :, t, own, :])
+    load_cot = load(4, lambda x: cot_h.at[:, :, :, x], lambda t: cot.at[:, :, :, lanes_of(t)])
+
+    def arrived(copies):
+        for copy in copies:
+            copy.wait()
 
     barrier = pltpu.get_barrier_semaphore()
     for step in range(1, groups):
@@ -267,19 +291,14 @@
 
     halo_a = Exchange(0, ja_send, ja_got, ka_send, ka_got)
 
-    def source_a(c, i, at):
-        if c < 3:
-            return prior[c, i, at : at + SUB, :]
-        return inv[i, at : at + SUB, :]
-
-    pack_rows4(source_a, ja_send, 4)
+    def source(c, i, at):
+        rows = slice(SUB + at, 2 * SUB + at)
+        return jnp.concatenate([va[c, i, t, rows, :] for t in range(tiles)], axis=1)
+
+    arrived(load_prior)
+    arrived(load_inv)
+    pack_rows4(source, ja_send, 4)
     halo_a.start_j()
-
-    @pl.loop(0, ni)
-    def _(i):
-        for c in range(3):
-            put(va, c, i, own, prior[c, i])
-        put(va, 3, i, own, inv[i])
 
     pack_lanes(va, ka_send, 4, SWEEPS)
     halo_a.start_k()
@@ -395,18 +414,25 @@
 
     halo_b = Exchange(2, jb_send, jb_got, kb_send, kb_got)
 
+    warp_out = []
+    for t in range(tiles):
+        warp_out.append(
+            pltpu.make_async_copy(
+                done.at[0:3, :, t, own, :], warp_h.at[:, :, :, lanes_of(t)], sem_out.at[t]
+            )
+        )
+        warp_out[-1].start()
+    arrived(load_offset)
+    arrived(load_vol)
+
     @pl.loop(0, ni)
     def _(i):
         for c in range(4):
             for t in range(tiles):
-                lanes = slice(t * LANES, (t + 1) * LANES)
+                value = sb[c, i, t, own, :]
                 if c < 3:
-                    value = done[c, i, t, own, :]
-                    warp_o[c, i, :, lanes] = value
-                    value = value + offset[c, i, :, lanes]
-                else:
-                    value = vol[i, :, lanes]
-                sb[c, i, t, own, :] = value
+                    value = value + done[c, i, t, own, :]
+                    sb[c, i, t, own, :] = value
                 jb_send[0, c, t, pl.ds(i, 1), :] = value[0:1]
                 jb_send[1, c, t, pl.ds(i, 1), :] = value[nj - 1 : nj]
 
@@ -447,6 +473,8 @@
         )
 
     low_i[...] = jnp.zeros(low_i.shape, f32)
+    arrived(load_cot)
+    arrived(warp_out)
     mine = slice(SWEEPS, SWEEPS + nj)
     _, wide_high = nearby(wide)
 
@@ -495,12 +523,7 @@
 
     halo_c = Exchange(4, jc_send, jc_got, kc_send, kc_got)
 
-    def source_c(c, i, at):
-        return jnp.concatenate(
-            [va[c, i, t, SUB + at : 2 * SUB + at, :] for t in range(tiles)], axis=1
-        )
-
-    pack_rows4(source_c, jc_send, 3)
+    pack_rows4(source, jc_send, 3)
     halo_c.start_j()
     pack_lanes(va, kc_send, 3, SWEEPS)
     halo_c.start_k()
@@ -630,6 +653,7 @@
         ]
 
     vmem = pl.BlockSpec(memory_space=pltpu.VMEM)
+    anywhere = pl.BlockSpec(memory_space=pl.ANY)
     outs = pl.pallas_call(
         functools.partial(kernel, groups, slabs),
         out_shape=(
@@ -637,8 +661,8 @@
             jax.ShapeDtypeStruct(offset.shape, f32),
             jax.ShapeDtypeStruct(struct_disp.shape, f32),
         ),
-        in_specs=[vmem] * 10,
-        out_specs=[vmem] * 3,
+        in_specs=[vmem] * 5 + [anywhere] * 5,
+        out_specs=[anywhere, vmem, vmem],
         scratch_shapes=[
             pltpu.VMEM((4, ni, tiles + 1, rows_k, LANES), f32),
             pltpu.VMEM((3, ni, tiles + 1, rows_k, LANES), f32),
@@ -659,6 +683,9 @@
             pltpu.SemaphoreType.DMA((2, groups)),
             pltpu.SemaphoreType.DMA((2, groups)),
             pltpu.SemaphoreType.DMA((2, 7, 4)),
+            pltpu.VMEM((3, ni, nj, nk), f32),
+            pltpu.SemaphoreType.DMA((5, tiles)),
+            pltpu.SemaphoreType.DMA((tiles,)),
         ],
         compiler_params=pltpu.CompilerParams(
             collective_id=0, has_side_effects=True, vmem_limit_bytes=VMEM_LIMIT

time: 81.4 us -> 75.1 us (0.923)
  local copies, waits for them, and re-layouts: 12.6 us -> 4.59 us
  Pallas kernels: 67.7 us -> 69.7 us
    unnamed x23 -> x7, local copies, waits for them, and re-layouts: 12.6 us -> 4.59 us
    pallas_call x1, Pallas kernels: 67.7 us -> 69.7 us  [body(): pl.pallas_call(functools.partial(kernel, groups, slabs), out_shape=(jax.S...]
where the time goes in v2:
time: 75.1 us; the launch traced here: 74.9 us
  Pallas kernels  69.7 us (93%)
  local copies, waits for them, and re-layouts  4.59 us (6%)
    pallas_call x1, Pallas kernels, body(): pl.pallas_call(functools.partial(kernel, groups, slabs), out_shape=(jax.S...  69.7 us
    unnamed x7, local copies, waits for them, and re-layouts  4.59 us

profile of v2, /device:TPU:3, one launch (start us, length us, event | category | flops | bytes accessed | tf_op | source)
XLA Modules:
  0.0 74.9 jit_solution(12408260435626872362)
XLA Ops:
  0.6 69.7 %warp_adjoint.1 = (f32[3,16,32,256]{3,2,1,0:T(8,128)}, f32[3,16,32,256]{3,2,1,0:T(8,128)}, f32[3,512]{1,0:T(4,128)}) custom-call(s32[512]{0:T(512)} %struct_of.1, s32[512]{0:T(512)} %bitcast.1, s32[512]{0:T(512)} %node_of.1, f32[512]{0:T(512)} %weight_of.1, f32[3,512]{1,0:T(4,128)} %disp.1, f32[3,16,32,256]{3,2,1,0:T(8,128)} %offset_h.1, ...), custom_call_target="tpu_custom_call" | custom-call | tf_op jit(solution)/shard_map/warp_adjoint/pallas_call | solution.py:657
  70.3 0.0 copy-start
  70.3 2.8 %copy.16 = f32[3,16,32,256]{3,2,1,0:T(8,128)} copy(f32[3,16,32,256]{3,2,1,0:T(8,128)} %get-tuple-element.6) | data formatting | bytes 3145728
  73.1 0.0 copy-done
  73.2 0.0 copy-start.1
  73.2 1.1 %copy.17 = f32[3,16,32,256]{3,2,1,0:T(8,128)} copy(f32[3,16,32,256]{3,2,1,0:T(8,128)S(1)} %copy-done) | data formatting | bytes 3145728
  74.3 0.0 copy-done.1
  74.3 0.6 copy.18
Async XLA Ops:
  70.3 2.9 %copy-start = (f32[3,16,32,256]{3,2,1,0:T(8,128)S(1)}, f32[3,16,32,256]{3,2,1,0:T(8,128)}, u32[]{:S(2)}) copy-start(f32[3,16,32,256]{3,2,1,0:T(8,128)} %get-tuple-element.7) | copy-start | bytes 4718596
  73.2 1.1 %copy-start.1 = (f32[3,512]{1,0:T(4,128)S(1)}, f32[3,512]{1,0:T(4,128)}, u32[]{:S(2)}) copy-start(f32[3,512]{1,0:T(4,128)} %get-tuple-element.8) | copy-start | bytes 18436

commit v3 on v2

--- a/solution.py
+++ b/solution.py
@@ -307,9 +307,6 @@
     row_of = (me * nj + row_p - SWEEPS).astype(f32)
     col_of = iota((nk, records), 0).astype(f32)
 
-    for step in range(1, groups):
-        rec_copy(step).wait_recv()
-
     def scatter(g, total):
         got = rec_got[g]
         here = row_of == got[3:4, :]
@@ -329,7 +326,12 @@
         rows = 3 * np_j
         return total + (out[0:rows] + out[rows : 2 * rows] + out[2 * rows :])
 
-    surface = lax.fori_loop(0, groups, scatter, jnp.zeros((3 * np_j, nk), f32))
+    def scatter_next(step, total):
+        rec_copy(step).wait_recv()
+        return scatter(lax.rem(me - step + groups, groups), total)
+
+    surface = scatter(me, jnp.zeros((3 * np_j, nk), f32))
+    surface = lax.fori_loop(1, groups, scatter_next, surface)
     for c in range(3):
         put(va, c, 0, slice(near, near + np_j), surface[c * np_j : (c + 1) * np_j])
 
@@ -396,10 +398,20 @@
 
     wide = slice(near, near + np_j)
 
+    def in_pairs(first, stop):
+        def run(step):
+            even = first + (stop - first) // 2 * 2
+            if even > first:
+                pl.loop(first, even, unroll=2)(step)
+            if even < stop:
+                step(even)
+
+        return run
+
     def sweep_a(src, dst, last):
         rows, count = (own, tiles) if last else (wide, tiles + 1)
 
-        @pl.loop(1, ni - 1)
+        @in_pairs(1, ni - 1)
         def _(i):
             for c in range(3):
                 x, change = changes(src, c, i, rows, count)
@@ -546,7 +558,7 @@
         rows, count = (own, tiles) if last else (wide, tiles + 1)
         kept = slice(0, nj) if last else mine
 
-        @pl.loop(first, stop)
+        @in_pairs(first, stop)
         def _(i):
             for c in range(3):
                 x, change = changes(src, c, i, rows, count)
@@ -583,8 +595,7 @@
             device_id_type=MESH,
         )
 
-    @pl.loop(0, groups)
-    def _(g):
+    def answer(g):
         got = rec_got[g]
         cols = (col_of == got[4:5, :]).astype(bf16)
         here = row_w == got[3:4, :]
@@ -599,8 +610,12 @@
             )
         reply_send[g, 3:8, :] = jnp.zeros((5, records), f32)
 
-    for step in range(1, groups):
+    @pl.loop(1, groups)
+    def _(step):
+        answer(lax.rem(me + step, groups))
         reply_copy(step).start()
+
+    answer(me)
     reply_got[me] = reply_send[me]
     for sweep in range(SWEEPS):
         add_wall(sweep, ni - 1, ni - 2)

time: 75.1 us -> 70.6 us (0.940)
  Pallas kernels: 69.7 us -> 65.1 us
    pallas_call x1, Pallas kernels: 69.7 us -> 65.1 us  [body(): pl.pallas_call(functools.partial(kernel, groups, slabs), out_shape=(jax.S...]
where the time goes in v3:
time: 70.6 us; the launch traced here: 70.4 us
  Pallas kernels  65.1 us (92%)
  local copies, waits for them, and re-layouts  4.59 us (7%)
    pallas_call x1, Pallas kernels, body(): pl.pallas_call(functools.partial(kernel, groups, slabs), out_shape=(jax.S...  65.1 us
    unnamed x7, local copies, waits for them, and re-layouts  4.59 us

profile of v3, /device:TPU:3, one launch (start us, length us, event | category | flops | bytes accessed | tf_op | source)
XLA Modules:
  0.0 70.4 jit_solution(2237702844296065150)
XLA Ops:
  0.6 65.1 %warp_adjoint.1 = (f32[3,16,32,256]{3,2,1,0:T(8,128)}, f32[3,16,32,256]{3,2,1,0:T(8,128)}, f32[3,512]{1,0:T(4,128)}) custom-call(s32[512]{0:T(512)} %struct_of.1, s32[512]{0:T(512)} %bitcast.1, s32[512]{0:T(512)} %node_of.1, f32[512]{0:T(512)} %weight_of.1, f32[3,512]{1,0:T(4,128)} %disp.1, f32[3,16,32,256]{3,2,1,0:T(8,128)} %offset_h.1, ...), custom_call_target="tpu_custom_call" | custom-call | tf_op jit(solution)/shard_map/warp_adjoint/pallas_call | solution.py:672
  65.8 0.0 copy-start
  65.8 2.8 %copy.16 = f32[3,16,32,256]{3,2,1,0:T(8,128)} copy(f32[3,16,32,256]{3,2,1,0:T(8,128)} %get-tuple-element.6) | data formatting | bytes 3145728
  68.6 0.0 copy-done
  68.6 0.0 copy-start.1
  68.6 1.1 %copy.17 = f32[3,16,32,256]{3,2,1,0:T(8,128)} copy(f32[3,16,32,256]{3,2,1,0:T(8,128)S(1)} %copy-done) | data formatting | bytes 3145728
  69.8 0.0 copy-done.1
  69.8 0.6 copy.18
Async XLA Ops:
  65.8 2.9 %copy-start = (f32[3,16,32,256]{3,2,1,0:T(8,128)S(1)}, f32[3,16,32,256]{3,2,1,0:T(8,128)}, u32[]{:S(2)}) copy-start(f32[3,16,32,256]{3,2,1,0:T(8,128)} %get-tuple-element.7) | copy-start | bytes 4718596
  68.6 1.1 %copy-start.1 = (f32[3,512]{1,0:T(4,128)S(1)}, f32[3,512]{1,0:T(4,128)}, u32[]{:S(2)}) copy-start(f32[3,512]{1,0:T(4,128)} %get-tuple-element.8) | copy-start | bytes 18436
